TPU v7x, 256 devices: a whole 4x4x8 slice. The times are simulated.
256 devices in a mesh: slab: 32 (over x, z_hi, y), head: 8 (over z_lo, core).
Axes of the slice: x: 4, y: 4, z: 8 (z_hi: 2, z_lo: 4; z = z_hi * 4 + z_lo), core: 2. Of those that a mesh axis runs over, the one named last changes fastest.
Arguments:
- inputs: bfloat16 [32768, 1024], P('slab'), may hold values from -6 to 6
- norm_gain: float32 [1024], replicated, may hold values from 0.1 to 1.9
- query_weight: bfloat16 [1024, 1024], P('slab', 'head'), may hold values from -0.1875 to 0.1875
- key_weight: bfloat16 [1024, 1024], P('slab', 'head'), may hold values from -0.1875 to 0.1875
- value_weight: bfloat16 [1024, 1024], P('slab', 'head'), may hold values from -0.1875 to 0.1875
- out_weight: bfloat16 [1024, 1024], P('head', 'slab'), may hold values from -0.1875 to 0.1875
- logit_scale: float32 [16], P('head'), may hold values from 0.5 to 4, as said below
- grad_output: bfloat16 [32768, 1024], P('slab'), may hold values from -6 to 6
Outputs:
- grad_inputs: bfloat16 [32768, 1024], P('slab', 'head')
- grad_gain: float32 [1024], P('head')
- grad_query_weight: float32 [1024, 1024], P('slab', 'head')
- grad_key_weight: float32 [1024, 1024], P('slab', 'head')
- grad_value_weight: float32 [1024, 1024], P('slab', 'head')
- grad_out_weight: float32 [1024, 1024], P('head', 'slab')
Inputs may be any that keep to these rules, and one draw needn't show every extreme that they name: `logit_scale`: positive multipliers of each head's attention logits.
All inputs are finite; a program needn't handle non-finite values.
Results may differ from a plain program's by a relative error of at most 0.015.
The roundings to bfloat16 on the way count: a program that leaves them out, or rounds other values in their place, can miss the bound.
Values may be sent and summed in bfloat16 or wider, within the bound.
No kernel may reach another device: no remote copies, remote signals or barrier semaphores. Data moves between devices by JAX's collectives and lax.ppermute only.
A program may use at most 128 MiB of HBM per device.

v0:
```python
import math
import jax
import jax.numpy as jnp
from jax import lax
from jax.sharding import PartitionSpec as P

NX = 32
NY = 32


def rows_first(arrays, axis, dims):
    turned = [jnp.moveaxis(a, dim, 0) for a, dim in zip(arrays, dims)]
    widths = [t[0].size for t in turned]
    both = jnp.concatenate([t.reshape(-1, w) for t, w in zip(turned, widths)], axis=1)
    whole = lax.all_gather(both, axis, axis=0, tiled=True)
    pieces = jnp.split(whole, [sum(widths[:k]) for k in range(1, len(widths))], axis=1)
    return tuple(
        (
            jnp.moveaxis(b.reshape(-1, *t.shape[1:]), 0, dim)
            for b, t, dim in zip(pieces, turned, dims)
        )
    )


def sent_together(arrays, axis, split_dim, concat_dim, along):
    both = jnp.concatenate(arrays, axis=along)
    whole, at, done = (
        lax.all_to_all(both, axis, split_axis=split_dim, concat_axis=concat_dim, tiled=True),
        0,
        [],
    )
    for a in arrays:
        done.append(lax.slice_in_dim(whole, at, at + a.shape[along], axis=along))
        at += a.shape[along]
    return tuple(done)


def shortened(x):

    def short(part):
        return part.astype(jnp.bfloat16) if part.dtype == jnp.float32 else part

    return jax.tree.map(short, x)


def split_up(x, dim, size):
    lengths = x.shape
    pieces = x.reshape(*lengths[:dim], size, lengths[dim] // size, *lengths[dim + 1 :])
    return jnp.moveaxis(pieces, dim, 0)


def summed_on_arrival(x, axis, dim):
    size = lax.axis_size(axis)
    pieces = lax.all_to_all(split_up(x, dim, size), axis, 0, 0, tiled=True)
    return jnp.sum(pieces.astype(jnp.float32), axis=0)


def sent_to_all(x, axis):
    size = lax.axis_size(axis)
    return lax.all_to_all(jnp.broadcast_to(x[None], (size, *x.shape)), axis, 0, 0, tiled=True)


def over_copies(x, axis):
    everything = sent_to_all(x, axis)
    return jnp.sum(everything, axis=0)


def summed_on_arrival_2(x, axis, dim):
    size = lax.axis_size(axis)
    pieces = lax.all_to_all(split_up(x, dim, size), axis, 0, 0, tiled=True)
    return jnp.sum(pieces, axis=0)


def line_attention(queries, key_rows, values, grad_attn, scale_factor):
    line_count, length, head_count, head_dim = queries.shape
    bundle = math.gcd(line_count, max(1, 128 // length))
    block_width = length * bundle
    blocks = line_count // bundle
    query_blocks, key_blocks, value_blocks, grad_blocks = tuple(
        (
            tensor.reshape(blocks, block_width, head_count, head_dim)
            for tensor in (queries, key_rows, values, grad_attn)
        )
    )
    position = jnp.arange(block_width) // length
    same_line = position[:, None] == position[None, :]
    factor = scale_factor[None, :, None, None]
    score_matrix = (
        jnp.einsum("bqhd,bkhd->bhqk", query_blocks, key_blocks, preferred_element_type=jnp.float32)
        * factor
    )
    score_matrix = jnp.where(same_line, score_matrix, -jnp.inf)
    highest = jnp.max(score_matrix, axis=-1, keepdims=True)
    exponent = jnp.exp(score_matrix - highest)
    softmax_p = exponent / jnp.sum(exponent, axis=-1, keepdims=True)
    rounded_probability = softmax_p.astype(jnp.bfloat16)
    output_rows = jnp.einsum(
        "bhqk,bkhd->bqhd", rounded_probability, value_blocks, preferred_element_type=jnp.float32
    )
    probability_gradient = jnp.einsum(
        "bqhd,bkhd->bhqk", grad_blocks, value_blocks, preferred_element_type=jnp.float32
    )
    row_delta = jnp.einsum("bqhd,bqhd->bhq", grad_blocks.astype(jnp.float32), output_rows)
    score_gradient = (softmax_p * (probability_gradient - row_delta[..., None]) * factor).astype(
        jnp.bfloat16
    )
    query_gradient = jnp.einsum(
        "bhqk,bkhd->bqhd", score_gradient, key_blocks, preferred_element_type=jnp.float32
    )
    key_gradient = jnp.einsum(
        "bhqk,bqhd->bkhd", score_gradient, query_blocks, preferred_element_type=jnp.float32
    )
    value_gradient = jnp.einsum(
        "bhqk,bqhd->bkhd", rounded_probability, grad_blocks, preferred_element_type=jnp.float32
    )
    return tuple(
        (
            result.reshape(line_count, length, head_count, head_dim)
            for result in (output_rows, query_gradient, key_gradient, value_gradient)
        )
    )


def local_axes(grids, scale_factor, head_dim):
    planes, rows_y, rows_x, head_width = grids[0].shape
    head_count = head_width // head_dim
    along_x = line_attention(
        *[grid.reshape(planes * rows_y, rows_x, head_count, head_dim) for grid in grids],
        scale_factor
    )
    along_x = [result.reshape(planes, rows_y, rows_x, head_width) for result in along_x]
    along_y = line_attention(
        *[
            jnp.transpose(grid, (0, 2, 1, 3)).reshape(planes * rows_x, rows_y, head_count, head_dim)
            for grid in grids
        ],
        scale_factor
    )
    along_y = [
        jnp.transpose(result.reshape(planes, rows_x, rows_y, head_width), (0, 2, 1, 3))
        for result in along_y
    ]
    return tuple((along_x[index] + along_y[index] for index in range(4)))


def z_lines(grids, scale_factor, head_dim):
    depth, rows_y, rows_x, head_width = grids[0].shape
    head_count = head_width // head_dim
    results = line_attention(
        *[
            jnp.transpose(grid, (1, 2, 0, 3)).reshape(rows_y * rows_x, depth, head_count, head_dim)
            for grid in grids
        ],
        scale_factor
    )
    return tuple(
        (
            jnp.transpose(result.reshape(rows_y, rows_x, depth, head_width), (2, 0, 1, 3)).astype(
                jnp.bfloat16
            )
            for result in results
        )
    )


def body(
    inputs, norm_gain, query_weight, key_weight, value_weight, out_weight, logit_scale, grad_output
):
    rows, width = inputs.shape
    head_width = query_weight.shape[1]
    head_dim = head_width // logit_scale.shape[0]
    slab_count = lax.axis_size("slab")
    share = width // lax.axis_size("head")
    loss_scale = 1.0 / math.sqrt(rows * slab_count)
    planes = rows // (NY * NX)
    features = inputs.astype(jnp.float32)
    inv_rms = lax.rsqrt(jnp.mean(features * features, axis=1) + 1e-06)
    normed = (features * inv_rms[:, None] * norm_gain[None, :]).astype(jnp.bfloat16)
    full_query, full_key, full_value, full_out = rows_first(
        (query_weight, key_weight, value_weight, out_weight), "slab", (0, 0, 0, 1)
    )
    queries = jnp.dot(normed, full_query, preferred_element_type=jnp.float32).astype(jnp.bfloat16)
    key_rows = jnp.dot(normed, full_key, preferred_element_type=jnp.float32).astype(jnp.bfloat16)
    values = jnp.dot(normed, full_value, preferred_element_type=jnp.float32).astype(jnp.bfloat16)
    grad_attn = lax.dot_general(
        grad_output, full_out, (((1,), (1,)), ((), ())), preferred_element_type=jnp.float32
    ).astype(jnp.bfloat16)
    scale_factor = logit_scale / math.sqrt(head_dim)
    grids = tuple(
        (
            array.reshape(planes, NY, NX, head_width)
            for array in (queries, key_rows, values, grad_attn)
        )
    )
    moved = sent_together((grids[0], grids[1], grids[2]), "slab", 1, 0, 2)
    moved_grad = lax.all_to_all(grids[3], "slab", split_axis=1, concat_axis=0, tiled=True)
    z_terms = z_lines((moved[0], moved[1], moved[2], moved_grad), scale_factor, head_dim)
    z_back = jax.tree.map(
        lambda part, own: part.astype(own.dtype),
        lax.all_to_all(shortened(z_terms), "slab", split_axis=0, concat_axis=1, tiled=True),
        z_terms,
    )
    local_terms = local_axes(grids, scale_factor, head_dim)
    combined = tuple(
        (
            (local_terms[index] + z_back[index].astype(jnp.float32))
            .astype(jnp.bfloat16)
            .reshape(rows, head_width)
            for index in range(4)
        )
    )
    attn, query_gradient, key_gradient, value_gradient = combined
    contract = (((1,), (1,)), ((), ()))
    partial_sum = lax.dot_general(
        query_gradient, full_query, contract, preferred_element_type=jnp.float32
    )
    partial_sum = partial_sum + lax.dot_general(
        key_gradient, full_key, contract, preferred_element_type=jnp.float32
    )
    partial_sum = partial_sum + lax.dot_general(
        value_gradient, full_value, contract, preferred_element_type=jnp.float32
    )
    partial_sum = partial_sum.astype(jnp.bfloat16)
    first_col = lax.axis_index("head") * share
    feature_share = lax.dynamic_slice_in_dim(features, first_col, share, 1)
    gain_share = lax.dynamic_slice_in_dim(norm_gain, first_col, share, 0)
    grad_normed = summed_on_arrival(partial_sum, "head", 1)
    row_dot = over_copies(
        jnp.sum(grad_normed * feature_share * gain_share[None, :], axis=1), "head"
    )
    grad_inputs = (
        inv_rms[:, None] * gain_share[None, :] * grad_normed
        - feature_share * (inv_rms**3)[:, None] * row_dot[:, None] / width
    ).astype(jnp.bfloat16)
    grad_gain = (
        over_copies(jnp.sum(grad_normed * feature_share * inv_rms[:, None], axis=0), "slab")
        * loss_scale
    )
    grads_stack = jnp.concatenate([query_gradient, key_gradient, value_gradient], axis=1)
    tokens_contract = (((0,), (0,)), ((), ()))
    inner = lax.dot_general(
        normed, grads_stack, tokens_contract, preferred_element_type=jnp.float32
    )
    outer = lax.dot_general(grad_output, attn, tokens_contract, preferred_element_type=jnp.float32)
    reduced = summed_on_arrival_2(jnp.concatenate([inner, outer], axis=1), "slab", 0) * loss_scale
    grad_query_weight = reduced[:, :head_width]
    grad_key_weight = reduced[:, head_width : 2 * head_width]
    grad_value_weight = reduced[:, 2 * head_width : 3 * head_width]
    grad_out_weight = reduced[:, 3 * head_width :].T
    return (
        grad_inputs,
        grad_gain,
        grad_query_weight,
        grad_key_weight,
        grad_value_weight,
        grad_out_weight,
    )


def solution(mesh):
    in_specs = (
        P("slab", None),
        P(),
        P("slab", "head"),
        P("slab", "head"),
        P("slab", "head"),
        P("head", "slab"),
        P("head"),
        P("slab", None),
    )
    out_specs = (
        P("slab", "head"),
        P("head"),
        P("slab", "head"),
        P("slab", "head"),
        P("slab", "head"),
        P("head", "slab"),
    )
    return jax.shard_map(body, mesh=mesh, in_specs=in_specs, out_specs=out_specs, check_vma=False)
```

profile of v0, /device:TPU:72, one launch (start us, length us, event | category | flops | bytes accessed | tf_op | source)
XLA Modules:
  0.0 466.1 jit_solution(10997156738980183589)
XLA Ops:
  8.8 4.0 copy.273
  12.8 2.2 multiply_reduce_fusion
  15.1 1.9 multiply_convert_fusion
  17.0 75.5 %all-gather.2.cloned.1.call-done = bf16[1024,512]{1,0:T(8,128)(2,1)} async-done(((bf16[32,512]{1,0:T(8,128)(2,1)}), bf16[1024,512]{1,0:T(8,128)(2,1)}) %all-gather.2.cloned.1.call-update) | async-done | bytes 1048592 | tf_op jit(solution)/shard_map/all_gather | solution.py:15
  92.5 1.8 convolution_convert_fusion.4
  98.8 2.4 convolution_convert_fusion.5
  103.6 2.4 convolution_convert_fusion.6
  108.3 3.0 convolution_convert_fusion.3
  111.3 2.1 reshape.205
  115.2 2.0 reshape_reshape.56
  117.2 1.9 copy.295
  120.3 2.7 fusion.65
  122.9 2.4 fusion.35
  125.4 1.8 fusion.19
  129.5 7.8 %all-to-all-start.1 = ((bf16[1,32,32,128]{3,2,0,1:T(8,128)(2,1)}), bf16[1,32,32,128]{3,2,0,1:T(8,128)(2,1)}, u32[]{:S(2)}, u32[]{:S(2)}) async-start(bf16[1,32,32,128]{3,2,0,1:T(8,128)(2,1)} %bitcast.29), calls=%async_computation.1 | async-start | bytes 524288 | tf_op jit(solution)/shard_map/all_to_all | solution.py:196
  138.6 2.0 copy.284
  141.3 1.9 copy.280
  144.2 2.7 convolution_bitcast_fusion.1
  148.4 2.6 all-to-all-done.1
  151.1 9.7 %all-to-all-start = ((bf16[1,32,96,128]{3,2,0,1:T(8,128)(2,1)}), bf16[1,32,96,128]{3,2,0,1:T(8,128)(2,1)S(1)}, u32[]{:S(2)}, u32[]{:S(2)}) async-start(bf16[1,32,96,128]{3,2,0,1:T(8,128)(2,1)} %pad_maximum_fusion.1), calls=%async_computation | async-start | bytes 1572864 | tf_op jit(solution)/shard_map/all_to_all | solution.py:28
  160.8 1.8 bitcast_convert_fusion.3
  162.6 2.6 fusion.36
  165.2 1.8 fusion.20
  174.7 2.1 copy.382
  176.8 7.7 %all-to-all-done = bf16[1,32,96,128]{3,2,0,1:T(8,128)(2,1)S(1)} async-done(((bf16[1,32,96,128]{3,2,0,1:T(8,128)(2,1)}), bf16[1,32,96,128]{3,2,0,1:T(8,128)(2,1)S(1)}, u32[]{:S(2)}, u32[]{:S(2)}) %all-to-all-start) | async-done | bytes 786464 | tf_op jit(solution)/shard_map/all_to_all | solution.py:28
  188.8 2.5 fusion.66
  192.8 1.9 fusion.34
  199.3 1.8 copy.333
  201.1 5.3 %all-to-all-start.3 = ((bf16[32,1,32,128]{3,2,1,0:T(8,128)(2,1)}), bf16[32,1,32,128]{3,2,1,0:T(8,128)(2,1)}, u32[]{:S(2)}, u32[]{:S(2)}) async-start(bf16[32,1,32,128]{3,2,1,0:T(8,128)(2,1)} %copy.333), calls=%async_computation.3 | async-start | bytes 524288 | tf_op jit(solution)/shard_map/all_to_all | solution.py:200
  206.4 2.6 convolution_bitcast_fusion.2
  210.4 1.8 reshape_reshape.65
  212.2 2.2 copy.337
  214.4 2.6 reshape_reshape.64
  217.0 2.2 copy.328
  219.2 2.6 reshape_reshape.63
  221.8 2.2 copy.325
  224.0 2.6 reshape_reshape.62
  226.7 2.2 copy.301
  228.8 2.7 reshape_reshape.57
  231.5 2.2 copy.286
  233.7 2.6 reshape_reshape.52
  244.6 2.0 copy.352
  248.7 12.3 %all-to-all-start.2 = ((bf16[32,1,32,128]{3,2,1,0:T(8,128)(2,1)}), bf16[32,1,32,128]{3,2,1,0:T(8,128)(2,1)}, u32[]{:S(2)}, u32[]{:S(2)}) async-start(bf16[32,1,32,128]{3,2,1,0:T(8,128)(2,1)} %copy.321), calls=%async_computation.2 | async-start | bytes 524288 | tf_op jit(solution)/shard_map/all_to_all | solution.py:200
  262.4 3.7 fusion.46
  266.1 8.1 %all-to-all-done.2 = bf16[32,1,32,128]{3,2,1,0:T(8,128)(2,1)} async-done(((bf16[32,1,32,128]{3,2,1,0:T(8,128)(2,1)}), bf16[32,1,32,128]{3,2,1,0:T(8,128)(2,1)}, u32[]{:S(2)}, u32[]{:S(2)}) %all-to-all-start.2) | async-done | bytes 262176 | tf_op jit(solution)/shard_map/all_to_all | solution.py:200
  274.2 5.3 %all-to-all-start.4 = ((bf16[32,1,32,128]{3,2,1,0:T(8,128)(2,1)}), bf16[32,1,32,128]{3,2,1,0:T(8,128)(2,1)}, u32[]{:S(2)}, u32[]{:S(2)}) async-start(bf16[32,1,32,128]{3,2,1,0:T(8,128)(2,1)} %copy.345), calls=%async_computation.4 | async-start | bytes 524288 | tf_op jit(solution)/shard_map/all_to_all | solution.py:200
  281.6 3.7 fusion.43
  285.3 6.5 %all-to-all-done.4 = bf16[32,1,32,128]{3,2,1,0:T(8,128)(2,1)} async-done(((bf16[32,1,32,128]{3,2,1,0:T(8,128)(2,1)}), bf16[32,1,32,128]{3,2,1,0:T(8,128)(2,1)}, u32[]{:S(2)}, u32[]{:S(2)}) %all-to-all-start.4) | async-done | bytes 262176 | tf_op jit(solution)/shard_map/all_to_all | solution.py:200
  291.9 5.9 %all-to-all-start.8 = ((bf16[32,1,32,128]{3,2,1,0:T(8,128)(2,1)}), bf16[32,1,32,128]{3,2,1,0:T(8,128)(2,1)}, u32[]{:S(2)}, u32[]{:S(2)}) async-start(bf16[32,1,32,128]{3,2,1,0:T(8,128)(2,1)} %copy.353), calls=%async_computation.8 | async-start | bytes 524288 | tf_op jit(solution)/shard_map/all_to_all | solution.py:200
  299.7 5.6 %add_convert_fusion = bf16[1024,1024]{0,1:T(8,128)(2,1)} fusion(f32[1024,1024]{0,1:T(8,128)} %fusion.43, f32[1024,1024]{0,1:T(8,128)} %fusion.46, bf16[1024,128]{1,0:T(8,128)(2,1)S(1)} %bitcast.227, bf16[1024,512]{1,0:T(8,128)(2,1)} %all-gather.2.cloned.1.call-done), kind=kOutput, calls=%fused_computation.4 | convolution fusion | flops 271581184 | bytes 11010048 | tf_op jit(solution)/shard_map/dot_general | solution.py:220
  305.3 4.7 %all-to-all-done.8 = bf16[32,1,32,128]{3,2,1,0:T(8,128)(2,1)} async-done(((bf16[32,1,32,128]{3,2,1,0:T(8,128)(2,1)}), bf16[32,1,32,128]{3,2,1,0:T(8,128)(2,1)}, u32[]{:S(2)}, u32[]{:S(2)}) %all-to-all-start.8) | async-done | bytes 262176 | tf_op jit(solution)/shard_map/all_to_all | solution.py:200
  310.0 4.5 all-to-all-start.5
  314.5 4.0 convert_element_type.164
  324.4 2.3 fusion.30
  326.7 3.9 fusion.24
  330.6 29.4 %all-to-all-done.5 = bf16[8,1024,128]{1,2,0:T(8,128)(2,1)} async-done(((bf16[8,1024,128]{1,2,0:T(8,128)(2,1)}), bf16[8,1024,128]{1,2,0:T(8,128)(2,1)}, u32[]{:S(2)}, u32[]{:S(2)}) %all-to-all-start.5) | async-done | bytes 2097184 | tf_op jit(solution)/shard_map/all_to_all | solution.py:54
  359.9 2.0 convert_reduce_fusion
  363.8 7.5 %all-to-all-start.7 = ((f32[32,1,128]{2,1,0:T(1,128)}), f32[32,1,128]{2,1,0:T(1,128)S(1)}, u32[]{:S(2)}, u32[]{:S(2)}) async-start(f32[32,1,128]{2,1,0:T(1,128)} %broadcast_in_dim.23), calls=%async_computation.7 | async-start | bytes 32768 | tf_op jit(solution)/shard_map/all_to_all | solution.py:60
  371.8 10.5 %all-to-all-done.7 = f32[32,1,128]{2,1,0:T(1,128)S(1)} async-done(((f32[32,1,128]{2,1,0:T(1,128)}), f32[32,1,128]{2,1,0:T(1,128)S(1)}, u32[]{:S(2)}, u32[]{:S(2)}) %all-to-all-start.7) | async-done | bytes 16416 | tf_op jit(solution)/shard_map/all_to_all | solution.py:60
  382.9 6.6 %all-to-all-start.6 = ((f32[8,1,1024]{2,1,0:T(1,128)}), f32[8,1,1024]{2,1,0:T(1,128)S(1)}, u32[]{:S(2)}, u32[]{:S(2)}) async-start(f32[8,1,1024]{2,1,0:T(1,128)} %broadcast_in_dim.22), calls=%async_computation.6 | async-start | bytes 65536 | tf_op jit(solution)/shard_map/all_to_all | solution.py:60
  389.5 3.0 pad_maximum_fusion
  392.5 2.9 copy.355
  395.4 5.8 %all-to-all-start.9 = ((f32[32,32,512]{2,1,0:T(8,128)}), f32[32,32,512]{2,1,0:T(8,128)}, u32[]{:S(2)}, u32[]{:S(2)}) async-start(f32[32,32,512]{2,1,0:T(8,128)} %bitcast.201), calls=%async_computation.9 | async-start | bytes 4194304 | tf_op jit(solution)/shard_map/all_to_all | solution.py:70
  403.8 53.1 %all-to-all-done.9 = f32[32,32,512]{2,1,0:T(8,128)} async-done(((f32[32,32,512]{2,1,0:T(8,128)}), f32[32,32,512]{2,1,0:T(8,128)}, u32[]{:S(2)}, u32[]{:S(2)}) %all-to-all-start.9) | async-done | bytes 2097184 | tf_op jit(solution)/shard_map/all_to_all | solution.py:70
  (152 shorter events, 69.6 us)
Async XLA Ops:
  7.2 85.3 %copy-start = (bf16[1024,1024]{1,0:T(8,128)(2,1)S(1)}, bf16[1024,1024]{1,0:T(8,128)(2,1)}, u32[]{:S(2)}) copy-start(bf16[1024,1024]{1,0:T(8,128)(2,1)} %param.15) | copy-start | bytes 6291460
  7.2 85.3 %all-gather.2.cloned.1.call-start = ((), (), s32[]{:S(2)}) async-start(), calls=%async_computation.10 | async-start | bytes 1081344 | tf_op jit(solution)/shard_map/all_gather | solution.py:15
  8.8 4.0 copy-start.34
  12.7 2.4 copy-start.1
  12.7 2.4 copy-start.33
  101.2 4.8 %copy-start.3 = (bf16[1024,128]{1,0:T(8,128)(2,1)}, bf16[1024,128]{1,0:T(8,128)(2,1)S(1)}, u32[]{:S(2)}) copy-start(bf16[1024,128]{1,0:T(8,128)(2,1)S(1)} %convolution_convert_fusion.5) | copy-start | bytes 786436
  105.9 2.4 copy-start.5
  111.3 7.7 %copy-start.2 = (f32[8,2,128,64]{3,1,2,0:T(2,128)S(1)}, f32[8,2,128,64]{3,1,2,0:T(2,128)}, u32[]{:S(2)}) copy-start(f32[8,2,128,64]{3,1,2,0:T(2,128)} %bitcast_convert_fusion.2) | copy-start | bytes 1572868
  120.2 2.7 copy-start.17
  120.2 2.7 copy-start.19
  120.3 2.7 copy-start.32
  128.4 14.8 %copy-start.4 = (bf16[1024,128]{1,0:T(8,128)(2,1)S(1)}, bf16[1024,128]{1,0:T(8,128)(2,1)}, u32[]{:S(2)}) copy-start(bf16[1024,128]{1,0:T(8,128)(2,1)} %copy-done.3) | copy-start | bytes 786436
  128.4 14.8 %copy-start.6 = (bf16[1024,128]{1,0:T(8,128)(2,1)S(1)}, bf16[1024,128]{1,0:T(8,128)(2,1)}, u32[]{:S(2)}) copy-start(bf16[1024,128]{1,0:T(8,128)(2,1)} %copy-done.5) | copy-start | bytes 786436
  128.4 14.8 %copy-start.7 = (bf16[1024,128]{1,0:T(8,128)(2,1)S(1)}, bf16[1024,128]{1,0:T(8,128)(2,1)}, u32[]{:S(2)}) copy-start(bf16[1024,128]{1,0:T(8,128)(2,1)} %convolution_convert_fusion.3) | copy-start | bytes 786436
  129.5 21.6 %all-to-all-start.1 = ((bf16[1,32,32,128]{3,2,0,1:T(8,128)(2,1)}), bf16[1,32,32,128]{3,2,0,1:T(8,128)(2,1)}, u32[]{:S(2)}, u32[]{:S(2)}) async-start(bf16[1,32,32,128]{3,2,0,1:T(8,128)(2,1)} %bitcast.29), calls=%async_computation.1 | async-start | bytes 524288 | tf_op jit(solution)/shard_map/all_to_all | solution.py:196
  138.6 8.3 %copy-start.13 = (bf16[8,128,2,64]{1,3,2,0:T(8,128)(2,1)}, bf16[8,128,2,64]{1,3,2,0:T(8,128)(2,1)S(1)}, u32[]{:S(2)}) copy-start(bf16[8,128,2,64]{1,3,2,0:T(8,128)(2,1)S(1)} %copy.276) | copy-start | bytes 786436
  141.3 2.9 copy-start.18
  144.2 2.7 copy-start.16
  148.4 14.2 %copy-start.14 = (bf16[8,128,2,64]{1,3,2,0:T(8,128)(2,1)S(1)}, bf16[8,128,2,64]{1,3,2,0:T(8,128)(2,1)}, u32[]{:S(2)}) copy-start(bf16[8,128,2,64]{1,3,2,0:T(8,128)(2,1)} %copy-done.13) | copy-start | bytes 786436
  151.1 33.4 %all-to-all-start = ((bf16[1,32,96,128]{3,2,0,1:T(8,128)(2,1)}), bf16[1,32,96,128]{3,2,0,1:T(8,128)(2,1)S(1)}, u32[]{:S(2)}, u32[]{:S(2)}) async-start(bf16[1,32,96,128]{3,2,0,1:T(8,128)(2,1)} %pad_maximum_fusion.1), calls=%async_computation | async-start | bytes 1572864 | tf_op jit(solution)/shard_map/all_to_all | solution.py:28
  185.3 1.3 copy-start.29
  185.3 2.1 copy-start.28
  187.4 3.9 copy-start.23
  187.8 5.0 %copy-start.11 = (f32[8,2,128,64]{2,3,1,0:T(8,128)S(1)}, f32[8,2,128,64]{2,3,1,0:T(8,128)}, u32[]{:S(2)}) copy-start(f32[8,2,128,64]{2,3,1,0:T(8,128)} %copy.382) | copy-start | bytes 1572868
  191.3 3.4 copy-start.20
  191.3 3.4 copy-start.21
  191.3 3.4 copy-start.27
  194.7 1.2 copy-start.26
  195.1 0.8 copy-start.12
  195.9 10.5 %copy-start.15 = (bf16[8,128,2,64]{1,3,2,0:T(8,128)(2,1)S(1)}, bf16[8,128,2,64]{1,3,2,0:T(8,128)(2,1)}, u32[]{:S(2)}) copy-start(bf16[8,128,2,64]{1,3,2,0:T(8,128)(2,1)} %copy-done.13) | copy-start | bytes 786436
  201.1 47.6 %all-to-all-start.3 = ((bf16[32,1,32,128]{3,2,1,0:T(8,128)(2,1)}), bf16[32,1,32,128]{3,2,1,0:T(8,128)(2,1)}, u32[]{:S(2)}, u32[]{:S(2)}) async-start(bf16[32,1,32,128]{3,2,1,0:T(8,128)(2,1)} %copy.333), calls=%async_computation.3 | async-start | bytes 524288 | tf_op jit(solution)/shard_map/all_to_all | solution.py:200
  206.4 2.7 copy-start.31
  228.8 7.5 %copy-start.22 = (bf16[8,128,2,64]{1,3,2,0:T(8,128)(2,1)S(1)}, bf16[8,128,2,64]{1,3,2,0:T(8,128)(2,1)}, u32[]{:S(2)}) copy-start(bf16[8,128,2,64]{1,3,2,0:T(8,128)(2,1)} %copy.313) | copy-start | bytes 786436
  242.4 18.6 %copy-start.10 = (f32[1,32,32,128]{3,2,1,0:T(8,128)S(1)}, f32[1,32,32,128]{3,2,1,0:T(8,128)}, u32[]{:S(2)}) copy-start(f32[1,32,32,128]{3,2,1,0:T(8,128)} %reshape_reshape.63) | copy-start | bytes 1572868
  248.7 25.5 %all-to-all-start.2 = ((bf16[32,1,32,128]{3,2,1,0:T(8,128)(2,1)}), bf16[32,1,32,128]{3,2,1,0:T(8,128)(2,1)}, u32[]{:S(2)}, u32[]{:S(2)}) async-start(bf16[32,1,32,128]{3,2,1,0:T(8,128)(2,1)} %copy.321), calls=%async_computation.2 | async-start | bytes 524288 | tf_op jit(solution)/shard_map/all_to_all | solution.py:200
  262.4 17.1 %copy-start.9 = (f32[1,32,32,128]{3,2,1,0:T(8,128)S(1)}, f32[1,32,32,128]{3,2,1,0:T(8,128)}, u32[]{:S(2)}) copy-start(f32[1,32,32,128]{3,2,1,0:T(8,128)} %reshape_reshape.57) | copy-start | bytes 1572868
  274.2 17.7 %all-to-all-start.4 = ((bf16[32,1,32,128]{3,2,1,0:T(8,128)(2,1)}), bf16[32,1,32,128]{3,2,1,0:T(8,128)(2,1)}, u32[]{:S(2)}, u32[]{:S(2)}) async-start(bf16[32,1,32,128]{3,2,1,0:T(8,128)(2,1)} %copy.345), calls=%async_computation.4 | async-start | bytes 524288 | tf_op jit(solution)/shard_map/all_to_all | solution.py:200
  280.9 0.7 copy-start.24
  281.6 16.1 %copy-start.8 = (f32[1,32,32,128]{3,2,1,0:T(8,128)S(1)}, f32[1,32,32,128]{3,2,1,0:T(8,128)}, u32[]{:S(2)}) copy-start(f32[1,32,32,128]{3,2,1,0:T(8,128)} %reshape_reshape.64) | copy-start | bytes 1572868
  291.9 18.1 %all-to-all-start.8 = ((bf16[32,1,32,128]{3,2,1,0:T(8,128)(2,1)}), bf16[32,1,32,128]{3,2,1,0:T(8,128)(2,1)}, u32[]{:S(2)}, u32[]{:S(2)}) async-start(bf16[32,1,32,128]{3,2,1,0:T(8,128)(2,1)} %copy.353), calls=%async_computation.8 | async-start | bytes 524288 | tf_op jit(solution)/shard_map/all_to_all | solution.py:200
  299.0 0.7 copy-start.25
  310.0 50.0 %all-to-all-start.5 = ((bf16[8,1024,128]{1,2,0:T(8,128)(2,1)}), bf16[8,1024,128]{1,2,0:T(8,128)(2,1)}, u32[]{:S(2)}, u32[]{:S(2)}) async-start(bf16[8,1024,128]{1,2,0:T(8,128)(2,1)} %bitcast.202), calls=%async_computation.5 | async-start | bytes 4194304 | tf_op jit(solution)/shard_map/all_to_all | solution.py:54
  330.6 40.7 %copy-start.30 = (bf16[1,32,32,128]{3,2,1,0:T(8,128)(2,1)S(1)}, bf16[1,32,32,128]{3,2,1,0:T(8,128)(2,1)}, u32[]{:S(2)}) copy-start(bf16[1,32,32,128]{3,2,1,0:T(8,128)(2,1)} %fusion.30) | copy-start | bytes 786436
  363.8 18.5 %all-to-all-start.7 = ((f32[32,1,128]{2,1,0:T(1,128)}), f32[32,1,128]{2,1,0:T(1,128)S(1)}, u32[]{:S(2)}, u32[]{:S(2)}) async-start(f32[32,1,128]{2,1,0:T(1,128)} %broadcast_in_dim.23), calls=%async_computation.7 | async-start | bytes 32768 | tf_op jit(solution)/shard_map/all_to_all | solution.py:60
  382.9 12.5 %all-to-all-start.6 = ((f32[8,1,1024]{2,1,0:T(1,128)}), f32[8,1,1024]{2,1,0:T(1,128)S(1)}, u32[]{:S(2)}, u32[]{:S(2)}) async-start(f32[8,1,1024]{2,1,0:T(1,128)} %broadcast_in_dim.22), calls=%async_computation.6 | async-start | bytes 65536 | tf_op jit(solution)/shard_map/all_to_all | solution.py:60
  395.4 61.5 %all-to-all-start.9 = ((f32[32,32,512]{2,1,0:T(8,128)}), f32[32,32,512]{2,1,0:T(8,128)}, u32[]{:S(2)}, u32[]{:S(2)}) async-start(f32[32,32,512]{2,1,0:T(8,128)} %bitcast.201), calls=%async_computation.9 | async-start | bytes 4194304 | tf_op jit(solution)/shard_map/all_to_all | solution.py:70
Sparse Core Ops, SparseCore 0:
  12.0 80.4 all-gather.1
where the time goes:
time: 469 us; the launch traced here: 466 us
  waiting for transfers between devices  198 us (42%)
  local copies, waits for them, and re-layouts  91.6 us (20%)
  starting transfers between devices  70.8 us (15%)
  matrix products  58.1 us (12%)
  other arithmetic  32.8 us (7%)
  between operations  14.7 us (3%)
    all_gather x1, waiting for transfers between devices, rows_first(): whole = lax.all_gather(both, axis, axis=0, tiled=True)  75.5 us
    all_to_all x1, waiting for transfers between devices, summed_on_arrival_2(): pieces = lax.all_to_all(split_up(x, dim, size), axis, 0, 0, tiled=True)  53.1 us
    all_to_all x1, waiting for transfers between devices, summed_on_arrival(): pieces = lax.all_to_all(split_up(x, dim, size), axis, 0, 0, tiled=True)  29.4 us
    all_to_all x4, starting transfers between devices, body(): lax.all_to_all(shortened(z_terms), 'slab', split_axis=0, concat_axis=1, t...  28.7 us
    another operation x22, local copies, waits for them, and re-layouts, line_attention(): tensor.reshape(blocks, block_width, head_count, head_dim)  22.1 us
    all_to_all x4, waiting for transfers between devices, body(): lax.all_to_all(shortened(z_terms), 'slab', split_axis=0, concat_axis=1, t...  19.3 us
    all_to_all x2, starting transfers between devices, sent_to_all(): lax.all_to_all(jnp.broadcast_to(x[None], (size, *x.shape)), axis, 0, 0, t...  14.2 us
    convert_element_type x12, local copies, waits for them, and re-layouts, z_lines(): jnp.transpose(result.reshape(rows_y, rows_x, depth, head_width), (2, 0, 1...  13.7 us
  transfers between devices with their start and end apart: 11, of which 9 were waited for; matrix products, arithmetic and copies ran while one was open for 26% of the time, Pallas kernels for 0%

commit v1 on v0

--- a/solution.py
+++ b/solution.py
@@ -12,7 +12,12 @@
     turned = [jnp.moveaxis(a, dim, 0) for a, dim in zip(arrays, dims)]
     widths = [t[0].size for t in turned]
     both = jnp.concatenate([t.reshape(-1, w) for t, w in zip(turned, widths)], axis=1)
-    whole = lax.all_gather(both, axis, axis=0, tiled=True)
+    whole = jnp.concatenate(
+        lax.all_to_all(
+            jnp.stack([both] * lax.axis_size(axis)), axis_name=axis, split_axis=0, concat_axis=0
+        ),
+        axis=0,
+    )
     pieces = jnp.split(whole, [sum(widths[:k]) for k in range(1, len(widths))], axis=1)
     return tuple(
         (

time: 469 us -> 411 us (0.88)
  waiting for transfers between devices: 198 us -> 141 us
  starting transfers between devices: 70.8 us -> 84.7 us
  between operations: 14.7 us -> 1.2 us
    all_gather x1 -> x0, waiting for transfers between devices: 75.5 us -> none  [rows_first(): whole = lax.all_gather(both, axis, axis=0, tiled=True)]
    all_to_all x0 -> x1, waiting for transfers between devices: none -> 23 us  [rows_first(): lax.all_to_all(jnp.stack([both] * lax.axis_size(axis)), axis_name=axis, s...]
    all_to_all x0 -> x1, starting transfers between devices: none -> 12.4 us  [rows_first(): lax.all_to_all(jnp.stack([both] * lax.axis_size(axis)), axis_name=axis, s...]
    unnamed x75 -> x83, local copies, waits for them, and re-layouts: 11.1 us -> 11.2 us
  transfers between devices with their start and end apart: 11 -> 11, of which waited for: 9 -> 9; matrix products, arithmetic and copies ran while one was open for 26% -> 28% of each run, Pallas kernels for 0% -> 0%
where the time goes in v1:
time: 411 us; the launch traced here: 409 us
  waiting for transfers between devices  141 us (34%)
  local copies, waits for them, and re-layouts  95 us (23%)
  starting transfers between devices  84.7 us (21%)
  matrix products  54.3 us (13%)
  other arithmetic  32.8 us (8%)
    all_to_all x1, waiting for transfers between devices, summed_on_arrival_2(): pieces = lax.all_to_all(split_up(x, dim, size), axis, 0, 0, tiled=True)  53.1 us
    all_to_all x4, starting transfers between devices, body(): lax.all_to_all(shortened(z_terms), 'slab', split_axis=0, concat_axis=1, t...  31.2 us
    all_to_all x1, waiting for transfers between devices, summed_on_arrival(): pieces = lax.all_to_all(split_up(x, dim, size), axis, 0, 0, tiled=True)  29.4 us
    another operation x22, local copies, waits for them, and re-layouts, line_attention(): tensor.reshape(blocks, block_width, head_count, head_dim)  25.7 us
    all_to_all x1, waiting for transfers between devices, rows_first(): lax.all_to_all(jnp.stack([both] * lax.axis_size(axis)), axis_name=axis, s...  23 us
    all_to_all x4, waiting for transfers between devices, body(): lax.all_to_all(shortened(z_terms), 'slab', split_axis=0, concat_axis=1, t...  19.9 us
    all_to_all x2, starting transfers between devices, sent_to_all(): lax.all_to_all(jnp.broadcast_to(x[None], (size, *x.shape)), axis, 0, 0, t...  14.5 us
    all_to_all x1, starting transfers between devices, rows_first(): lax.all_to_all(jnp.stack([both] * lax.axis_size(axis)), axis_name=axis, s...  12.4 us
  transfers between devices with their start and end apart: 11, of which 9 were waited for; matrix products, arithmetic and copies ran while one was open for 28% of the time, Pallas kernels for 0%

profile of v1, /device:TPU:72, one launch (start us, length us, event | category | flops | bytes accessed | tf_op | source)
XLA Modules:
  0.0 408.8 jit_solution(6394064291323753247)
XLA Ops:
  2.6 12.4 %all-to-all-start = ((bf16[32,32,512]{2,1,0:T(8,128)(2,1)}), bf16[32,32,512]{2,1,0:T(8,128)(2,1)S(1)}, u32[]{:S(2)}, u32[]{:S(2)}) async-start(bf16[32,32,512]{2,1,0:T(8,128)(2,1)} %stack.2), calls=%async_computation | async-start | bytes 2097152 | tf_op jit(solution)/shard_map/all_to_all | solution.py:16
  15.0 4.0 copy.273
  19.0 2.2 multiply_reduce_fusion
  21.3 1.9 multiply_convert_fusion
  23.2 23.0 %all-to-all-done = bf16[32,32,512]{2,1,0:T(8,128)(2,1)S(1)} async-done(((bf16[32,32,512]{2,1,0:T(8,128)(2,1)}), bf16[32,32,512]{2,1,0:T(8,128)(2,1)S(1)}, u32[]{:S(2)}, u32[]{:S(2)}) %all-to-all-start) | async-done | bytes 1048608 | tf_op jit(solution)/shard_map/all_to_all | solution.py:16
  46.2 3.5 convolution_convert_fusion.5
  63.9 2.1 reshape_reshape.53
  66.1 1.9 copy.299
  67.9 2.0 reshape.211
  69.9 1.8 copy.410
  71.7 2.0 reshape_reshape.56
  73.7 1.9 copy.295
  76.7 2.6 fusion.65
  79.4 2.4 fusion.35
  81.8 1.8 fusion.19
  86.0 5.2 %all-to-all-start.2 = ((bf16[1,32,32,128]{3,2,0,1:T(8,128)(2,1)}), bf16[1,32,32,128]{3,2,0,1:T(8,128)(2,1)}, u32[]{:S(2)}, u32[]{:S(2)}) async-start(bf16[1,32,32,128]{3,2,0,1:T(8,128)(2,1)} %bitcast.30), calls=%async_computation.2 | async-start | bytes 524288 | tf_op jit(solution)/shard_map/all_to_all | solution.py:201
  92.5 2.0 copy.284
  95.2 1.9 copy.280
  98.1 2.6 convolution_bitcast_fusion.1
  103.5 11.1 %all-to-all-start.1 = ((bf16[1,32,96,128]{3,2,0,1:T(8,128)(2,1)}), bf16[1,32,96,128]{3,2,0,1:T(8,128)(2,1)S(1)}, u32[]{:S(2)}, u32[]{:S(2)}) async-start(bf16[1,32,96,128]{3,2,0,1:T(8,128)(2,1)} %pad_maximum_fusion.1), calls=%async_computation.1 | async-start | bytes 1572864 | tf_op jit(solution)/shard_map/all_to_all | solution.py:33
  114.6 1.8 bitcast_convert_fusion.3
  116.4 2.6 fusion.36
  119.0 1.8 fusion.20
  123.1 1.8 copy.311
  128.4 2.1 copy.382
  130.6 3.9 all-to-all-done.1
  138.8 2.5 fusion.66
  142.7 1.9 fusion.34
  149.3 1.8 copy.333
  151.1 8.3 %all-to-all-start.4 = ((bf16[32,1,32,128]{3,2,1,0:T(8,128)(2,1)}), bf16[32,1,32,128]{3,2,1,0:T(8,128)(2,1)}, u32[]{:S(2)}, u32[]{:S(2)}) async-start(bf16[32,1,32,128]{3,2,1,0:T(8,128)(2,1)} %copy.333), calls=%async_computation.4 | async-start | bytes 524288 | tf_op jit(solution)/shard_map/all_to_all | solution.py:205
  159.4 2.6 convolution_bitcast_fusion.2
  163.3 2.7 reshape_reshape.65
  166.0 2.2 copy.337
  168.2 2.7 reshape_reshape.64
  172.1 2.7 reshape_reshape.63
  174.8 2.2 copy.325
  177.0 2.6 reshape_reshape.62
  180.9 2.7 reshape_reshape.57
  183.6 2.2 copy.286
  185.8 2.7 reshape_reshape.52
  192.0 2.0 fusion.21
  199.5 12.3 %all-to-all-start.3 = ((bf16[32,1,32,128]{3,2,1,0:T(8,128)(2,1)}), bf16[32,1,32,128]{3,2,1,0:T(8,128)(2,1)}, u32[]{:S(2)}, u32[]{:S(2)}) async-start(bf16[32,1,32,128]{3,2,1,0:T(8,128)(2,1)} %copy.321), calls=%async_computation.3 | async-start | bytes 524288 | tf_op jit(solution)/shard_map/all_to_all | solution.py:205
  213.4 2.7 fusion.46
  216.0 8.0 %all-to-all-done.3 = bf16[32,1,32,128]{3,2,1,0:T(8,128)(2,1)} async-done(((bf16[32,1,32,128]{3,2,1,0:T(8,128)(2,1)}), bf16[32,1,32,128]{3,2,1,0:T(8,128)(2,1)}, u32[]{:S(2)}, u32[]{:S(2)}) %all-to-all-start.3) | async-done | bytes 262176 | tf_op jit(solution)/shard_map/all_to_all | solution.py:205
  224.0 5.3 %all-to-all-start.5 = ((bf16[32,1,32,128]{3,2,1,0:T(8,128)(2,1)}), bf16[32,1,32,128]{3,2,1,0:T(8,128)(2,1)}, u32[]{:S(2)}, u32[]{:S(2)}) async-start(bf16[32,1,32,128]{3,2,1,0:T(8,128)(2,1)} %copy.345), calls=%async_computation.5 | async-start | bytes 524288 | tf_op jit(solution)/shard_map/all_to_all | solution.py:205
  231.6 2.7 fusion.43
  234.3 7.3 %all-to-all-done.5 = bf16[32,1,32,128]{3,2,1,0:T(8,128)(2,1)} async-done(((bf16[32,1,32,128]{3,2,1,0:T(8,128)(2,1)}), bf16[32,1,32,128]{3,2,1,0:T(8,128)(2,1)}, u32[]{:S(2)}, u32[]{:S(2)}) %all-to-all-start.5) | async-done | bytes 262176 | tf_op jit(solution)/shard_map/all_to_all | solution.py:205
  241.7 5.3 %all-to-all-start.9 = ((bf16[32,1,32,128]{3,2,1,0:T(8,128)(2,1)}), bf16[32,1,32,128]{3,2,1,0:T(8,128)(2,1)}, u32[]{:S(2)}, u32[]{:S(2)}) async-start(bf16[32,1,32,128]{3,2,1,0:T(8,128)(2,1)} %copy.353), calls=%async_computation.9 | async-start | bytes 524288 | tf_op jit(solution)/shard_map/all_to_all | solution.py:205
  249.3 5.5 %add_convert_fusion = bf16[1024,1024]{0,1:T(8,128)(2,1)} fusion(f32[1024,1024]{0,1:T(8,128)} %fusion.43, f32[1024,1024]{0,1:T(8,128)} %fusion.46, bf16[1024,128]{1,0:T(8,128)(2,1)S(1)} %bitcast.235, bf16[1024,512]{1,0:T(8,128)(2,1)S(1)} %bitcast.210), kind=kOutput, calls=%fused_computation.4 | convolution fusion | flops 271581184 | bytes 11010048 | tf_op jit(solution)/shard_map/dot_general | solution.py:225
  254.8 4.5 %all-to-all-done.9 = bf16[32,1,32,128]{3,2,1,0:T(8,128)(2,1)} async-done(((bf16[32,1,32,128]{3,2,1,0:T(8,128)(2,1)}), bf16[32,1,32,128]{3,2,1,0:T(8,128)(2,1)}, u32[]{:S(2)}, u32[]{:S(2)}) %all-to-all-start.9) | async-done | bytes 262176 | tf_op jit(solution)/shard_map/all_to_all | solution.py:205
  259.3 4.5 %all-to-all-start.6 = ((bf16[8,1024,128]{1,2,0:T(8,128)(2,1)}), bf16[8,1024,128]{1,2,0:T(8,128)(2,1)}, u32[]{:S(2)}, u32[]{:S(2)}) async-start(bf16[8,1024,128]{1,2,0:T(8,128)(2,1)} %bitcast.203), calls=%async_computation.6 | async-start | bytes 4194304 | tf_op jit(solution)/shard_map/all_to_all | solution.py:59
  263.8 4.0 convert_element_type.164
  273.7 2.3 fusion.30
  276.0 3.9 fusion.24
  279.9 29.4 %all-to-all-done.6 = bf16[8,1024,128]{1,2,0:T(8,128)(2,1)} async-done(((bf16[8,1024,128]{1,2,0:T(8,128)(2,1)}), bf16[8,1024,128]{1,2,0:T(8,128)(2,1)}, u32[]{:S(2)}, u32[]{:S(2)}) %all-to-all-start.6) | async-done | bytes 2097184 | tf_op jit(solution)/shard_map/all_to_all | solution.py:59
  309.2 2.0 convert_reduce_fusion
  313.1 7.8 %all-to-all-start.8 = ((f32[32,1,128]{2,1,0:T(1,128)}), f32[32,1,128]{2,1,0:T(1,128)S(1)}, u32[]{:S(2)}, u32[]{:S(2)}) async-start(f32[32,1,128]{2,1,0:T(1,128)} %broadcast_in_dim.23), calls=%async_computation.8 | async-start | bytes 32768 | tf_op jit(solution)/shard_map/all_to_all | solution.py:65
  321.4 10.5 %all-to-all-done.8 = f32[32,1,128]{2,1,0:T(1,128)S(1)} async-done(((f32[32,1,128]{2,1,0:T(1,128)}), f32[32,1,128]{2,1,0:T(1,128)S(1)}, u32[]{:S(2)}, u32[]{:S(2)}) %all-to-all-start.8) | async-done | bytes 16416 | tf_op jit(solution)/shard_map/all_to_all | solution.py:65
  332.5 6.6 %all-to-all-start.7 = ((f32[8,1,1024]{2,1,0:T(1,128)}), f32[8,1,1024]{2,1,0:T(1,128)S(1)}, u32[]{:S(2)}, u32[]{:S(2)}) async-start(f32[8,1,1024]{2,1,0:T(1,128)} %broadcast_in_dim.22), calls=%async_computation.7 | async-start | bytes 65536 | tf_op jit(solution)/shard_map/all_to_all | solution.py:65
  339.1 3.0 pad_maximum_fusion
  342.1 2.9 copy.355
  345.0 5.8 %all-to-all-start.10 = ((f32[32,32,512]{2,1,0:T(8,128)}), f32[32,32,512]{2,1,0:T(8,128)}, u32[]{:S(2)}, u32[]{:S(2)}) async-start(f32[32,32,512]{2,1,0:T(8,128)} %bitcast.202), calls=%async_computation.10 | async-start | bytes 4194304 | tf_op jit(solution)/shard_map/all_to_all | solution.py:75
  353.4 53.1 %all-to-all-done.10 = f32[32,32,512]{2,1,0:T(8,128)} async-done(((f32[32,32,512]{2,1,0:T(8,128)}), f32[32,32,512]{2,1,0:T(8,128)}, u32[]{:S(2)}, u32[]{:S(2)}) %all-to-all-start.10) | async-done | bytes 2097184 | tf_op jit(solution)/shard_map/all_to_all | solution.py:75
  406.5 1.7 reduce_sum.99
  (160 shorter events, 72.7 us)
Async XLA Ops:
  0.6 52.1 %copy-start = (bf16[1024,1024]{1,0:T(8,128)(2,1)S(1)}, bf16[1024,1024]{1,0:T(8,128)(2,1)}, u32[]{:S(2)}) copy-start(bf16[1024,1024]{1,0:T(8,128)(2,1)} %param.15) | copy-start | bytes 6291460
  2.6 43.6 %all-to-all-start = ((bf16[32,32,512]{2,1,0:T(8,128)(2,1)}), bf16[32,32,512]{2,1,0:T(8,128)(2,1)S(1)}, u32[]{:S(2)}, u32[]{:S(2)}) async-start(bf16[32,32,512]{2,1,0:T(8,128)(2,1)} %stack.2), calls=%async_computation | async-start | bytes 2097152 | tf_op jit(solution)/shard_map/all_to_all | solution.py:16
  15.0 4.0 copy-start.38
  19.0 2.3 copy-start.1
  19.0 2.4 copy-start.37
  46.2 6.5 %copy-start.2 = (bf16[32,32,512]{2,1,0:T(8,128)(2,1)}, bf16[32,32,512]{2,1,0:T(8,128)(2,1)S(1)}, u32[]{:S(2)}) copy-start(bf16[32,32,512]{2,1,0:T(8,128)(2,1)S(1)} %all-to-all-done) | copy-start | bytes 3145732
  46.2 3.5 copy-start.13
  53.5 4.5 %copy-start.5 = (bf16[1024,128]{1,0:T(8,128)(2,1)S(1)}, bf16[1024,128]{1,0:T(8,128)(2,1)}, u32[]{:S(2)}) copy-start(bf16[1024,128]{1,0:T(8,128)(2,1)} %convolution_convert_fusion.5) | copy-start | bytes 786436
  56.7 5.4 %copy-start.7 = (bf16[1024,128]{1,0:T(8,128)(2,1)S(1)}, bf16[1024,128]{1,0:T(8,128)(2,1)}, u32[]{:S(2)}) copy-start(bf16[1024,128]{1,0:T(8,128)(2,1)} %convolution_convert_fusion.6) | copy-start | bytes 786436
  63.9 11.6 %copy-start.4 = (f32[8,2,128,64]{3,1,2,0:T(2,128)S(1)}, f32[8,2,128,64]{3,1,2,0:T(2,128)}, u32[]{:S(2)}) copy-start(f32[8,2,128,64]{3,1,2,0:T(2,128)} %bitcast_convert_fusion.2) | copy-start | bytes 1572868
  76.7 2.6 copy-start.20
  76.7 2.6 copy-start.22
  76.7 2.6 copy-start.36
  84.9 12.2 %copy-start.6 = (bf16[1024,128]{1,0:T(8,128)(2,1)S(1)}, bf16[1024,128]{1,0:T(8,128)(2,1)}, u32[]{:S(2)}) copy-start(bf16[1024,128]{1,0:T(8,128)(2,1)} %convolution_convert_fusion.5) | copy-start | bytes 786436
  84.9 12.2 %copy-start.8 = (bf16[1024,128]{1,0:T(8,128)(2,1)S(1)}, bf16[1024,128]{1,0:T(8,128)(2,1)}, u32[]{:S(2)}) copy-start(bf16[1024,128]{1,0:T(8,128)(2,1)} %convolution_convert_fusion.6) | copy-start | bytes 786436
  84.9 12.3 %copy-start.9 = (bf16[1024,128]{1,0:T(8,128)(2,1)S(1)}, bf16[1024,128]{1,0:T(8,128)(2,1)}, u32[]{:S(2)}) copy-start(bf16[1024,128]{1,0:T(8,128)(2,1)} %convolution_convert_fusion.3) | copy-start | bytes 786436
  86.0 17.5 %all-to-all-start.2 = ((bf16[1,32,32,128]{3,2,0,1:T(8,128)(2,1)}), bf16[1,32,32,128]{3,2,0,1:T(8,128)(2,1)}, u32[]{:S(2)}, u32[]{:S(2)}) async-start(bf16[1,32,32,128]{3,2,0,1:T(8,128)(2,1)} %bitcast.30), calls=%async_computation.2 | async-start | bytes 524288 | tf_op jit(solution)/shard_map/all_to_all | solution.py:201
  92.5 8.3 %copy-start.16 = (bf16[8,128,2,64]{1,3,2,0:T(8,128)(2,1)}, bf16[8,128,2,64]{1,3,2,0:T(8,128)(2,1)S(1)}, u32[]{:S(2)}) copy-start(bf16[8,128,2,64]{1,3,2,0:T(8,128)(2,1)S(1)} %copy.276) | copy-start | bytes 786436
  95.2 2.9 copy-start.21
  98.1 2.7 copy-start.19
  102.3 14.1 %copy-start.17 = (bf16[8,128,2,64]{1,3,2,0:T(8,128)(2,1)S(1)}, bf16[8,128,2,64]{1,3,2,0:T(8,128)(2,1)}, u32[]{:S(2)}) copy-start(bf16[8,128,2,64]{1,3,2,0:T(8,128)(2,1)} %copy-done.16) | copy-start | bytes 786436
  103.5 31.0 %all-to-all-start.1 = ((bf16[1,32,96,128]{3,2,0,1:T(8,128)(2,1)}), bf16[1,32,96,128]{3,2,0,1:T(8,128)(2,1)S(1)}, u32[]{:S(2)}, u32[]{:S(2)}) async-start(bf16[1,32,96,128]{3,2,0,1:T(8,128)(2,1)} %pad_maximum_fusion.1), calls=%async_computation.1 | async-start | bytes 1572864 | tf_op jit(solution)/shard_map/all_to_all | solution.py:33
  135.3 1.3 copy-start.33
  135.3 2.1 copy-start.32
  137.4 3.8 copy-start.26
  137.8 5.0 %copy-start.10 = (f32[8,2,128,64]{2,3,1,0:T(8,128)S(1)}, f32[8,2,128,64]{2,3,1,0:T(8,128)}, u32[]{:S(2)}) copy-start(f32[8,2,128,64]{2,3,1,0:T(8,128)} %copy.382) | copy-start | bytes 1572868
  141.2 3.4 copy-start.23
  141.2 3.4 copy-start.24
  141.2 3.4 copy-start.31
  144.7 1.2 copy-start.30
  145.1 0.8 copy-start.14
  145.9 13.5 %copy-start.18 = (bf16[8,128,2,64]{1,3,2,0:T(8,128)(2,1)S(1)}, bf16[8,128,2,64]{1,3,2,0:T(8,128)(2,1)}, u32[]{:S(2)}) copy-start(bf16[8,128,2,64]{1,3,2,0:T(8,128)(2,1)} %copy-done.16) | copy-start | bytes 786436
  151.1 48.4 %all-to-all-start.4 = ((bf16[32,1,32,128]{3,2,1,0:T(8,128)(2,1)}), bf16[32,1,32,128]{3,2,1,0:T(8,128)(2,1)}, u32[]{:S(2)}, u32[]{:S(2)}) async-start(bf16[32,1,32,128]{3,2,1,0:T(8,128)(2,1)} %copy.333), calls=%async_computation.4 | async-start | bytes 524288 | tf_op jit(solution)/shard_map/all_to_all | solution.py:205
  159.4 2.6 copy-start.35
  163.3 7.5 %copy-start.12 = (f32[8,128,2,64]{1,3,2,0:T(8,128)S(1)}, f32[8,128,2,64]{1,3,2,0:T(8,128)}, u32[]{:S(2)}) copy-start(f32[8,128,2,64]{1,3,2,0:T(8,128)} %convolution_bitcast_fusion.3) | copy-start | bytes 1572868
  172.1 7.5 %copy-start.11 = (f32[8,128,2,64]{1,3,2,0:T(8,128)S(1)}, f32[8,128,2,64]{1,3,2,0:T(8,128)}, u32[]{:S(2)}) copy-start(f32[8,128,2,64]{1,3,2,0:T(8,128)} %convolution_bitcast_fusion.5) | copy-start | bytes 1572868
  180.9 7.5 %copy-start.25 = (bf16[8,128,2,64]{1,3,2,0:T(8,128)(2,1)S(1)}, bf16[8,128,2,64]{1,3,2,0:T(8,128)(2,1)}, u32[]{:S(2)}) copy-start(bf16[8,128,2,64]{1,3,2,0:T(8,128)(2,1)} %copy.313) | copy-start | bytes 786436
  185.8 6.2 %copy-start.15 = (bf16[8,2,128,128]{2,3,1,0:T(8,128)(2,1)S(1)}, bf16[8,2,128,128]{2,3,1,0:T(8,128)(2,1)}, u32[]{:S(2)}) copy-start(bf16[8,2,128,128]{2,3,1,0:T(8,128)(2,1)} %copy-done.14) | copy-start | bytes 1572868
  192.0 4.3 %copy-start.27 = (bf16[8,2,64,128]{3,2,1,0:T(8,128)(2,1)S(1)}, bf16[8,2,64,128]{3,2,1,0:T(8,128)(2,1)}, u32[]{:S(2)}) copy-start(bf16[8,2,64,128]{3,2,1,0:T(8,128)(2,1)} %get-tuple-element.46) | copy-start | bytes 786436
  196.3 17.1 %copy-start.3 = (bf16[32,32,512]{2,1,0:T(8,128)(2,1)S(1)}, bf16[32,32,512]{2,1,0:T(8,128)(2,1)}, u32[]{:S(2)}) copy-start(bf16[32,32,512]{2,1,0:T(8,128)(2,1)} %copy-done.2) | copy-start | bytes 3145732
  199.5 24.6 %all-to-all-start.3 = ((bf16[32,1,32,128]{3,2,1,0:T(8,128)(2,1)}), bf16[32,1,32,128]{3,2,1,0:T(8,128)(2,1)}, u32[]{:S(2)}, u32[]{:S(2)}) async-start(bf16[32,1,32,128]{3,2,1,0:T(8,128)(2,1)} %copy.321), calls=%async_computation.3 | async-start | bytes 524288 | tf_op jit(solution)/shard_map/all_to_all | solution.py:205
  224.0 17.6 %all-to-all-start.5 = ((bf16[32,1,32,128]{3,2,1,0:T(8,128)(2,1)}), bf16[32,1,32,128]{3,2,1,0:T(8,128)(2,1)}, u32[]{:S(2)}, u32[]{:S(2)}) async-start(bf16[32,1,32,128]{3,2,1,0:T(8,128)(2,1)} %copy.345), calls=%async_computation.5 | async-start | bytes 524288 | tf_op jit(solution)/shard_map/all_to_all | solution.py:205
  231.0 0.7 copy-start.28
  241.7 17.6 %all-to-all-start.9 = ((bf16[32,1,32,128]{3,2,1,0:T(8,128)(2,1)}), bf16[32,1,32,128]{3,2,1,0:T(8,128)(2,1)}, u32[]{:S(2)}, u32[]{:S(2)}) async-start(bf16[32,1,32,128]{3,2,1,0:T(8,128)(2,1)} %copy.353), calls=%async_computation.9 | async-start | bytes 524288 | tf_op jit(solution)/shard_map/all_to_all | solution.py:205
  248.6 0.7 copy-start.29
  259.3 50.0 %all-to-all-start.6 = ((bf16[8,1024,128]{1,2,0:T(8,128)(2,1)}), bf16[8,1024,128]{1,2,0:T(8,128)(2,1)}, u32[]{:S(2)}, u32[]{:S(2)}) async-start(bf16[8,1024,128]{1,2,0:T(8,128)(2,1)} %bitcast.203), calls=%async_computation.6 | async-start | bytes 4194304 | tf_op jit(solution)/shard_map/all_to_all | solution.py:59
  279.9 41.0 %copy-start.34 = (bf16[1,32,32,128]{3,2,1,0:T(8,128)(2,1)S(1)}, bf16[1,32,32,128]{3,2,1,0:T(8,128)(2,1)}, u32[]{:S(2)}) copy-start(bf16[1,32,32,128]{3,2,1,0:T(8,128)(2,1)} %fusion.30) | copy-start | bytes 786436
  313.1 18.8 %all-to-all-start.8 = ((f32[32,1,128]{2,1,0:T(1,128)}), f32[32,1,128]{2,1,0:T(1,128)S(1)}, u32[]{:S(2)}, u32[]{:S(2)}) async-start(f32[32,1,128]{2,1,0:T(1,128)} %broadcast_in_dim.23), calls=%async_computation.8 | async-start | bytes 32768 | tf_op jit(solution)/shard_map/all_to_all | solution.py:65
  332.5 12.5 %all-to-all-start.7 = ((f32[8,1,1024]{2,1,0:T(1,128)}), f32[8,1,1024]{2,1,0:T(1,128)S(1)}, u32[]{:S(2)}, u32[]{:S(2)}) async-start(f32[8,1,1024]{2,1,0:T(1,128)} %broadcast_in_dim.22), calls=%async_computation.7 | async-start | bytes 65536 | tf_op jit(solution)/shard_map/all_to_all | solution.py:65
  345.0 61.5 %all-to-all-start.10 = ((f32[32,32,512]{2,1,0:T(8,128)}), f32[32,32,512]{2,1,0:T(8,128)}, u32[]{:S(2)}, u32[]{:S(2)}) async-start(f32[32,32,512]{2,1,0:T(8,128)} %bitcast.202), calls=%async_computation.10 | async-start | bytes 4194304 | tf_op jit(solution)/shard_map/all_to_all | solution.py:75
